TPU v7x, 256 devices: a whole 4x4x8 slice. The times are simulated.
256 devices in a mesh: node: 32 (over x, z_lo, core), local: 8 (over z_hi, y).
Axes of the slice: x: 4, y: 4, z: 8 (z_hi: 2, z_lo: 4; z = z_hi * 4 + z_lo), core: 2. Of those that a mesh axis runs over, the one named last changes fastest.
Arguments:
- grad_values: bfloat16 [256, 8192, 512], P(('node', 'local')), may hold values from -4 to 4
- grad_exponents: int32 [256, 4, 8192], P(('node', 'local')), may hold values from -1 to 2
- proj: float32 [8192, 256], P(('local', 'node')), may hold values from -1.5 to 1.5
- weights: float32 [8192, 512], P(('local', 'node')), may hold values from -4 to 4
- moment1: float32 [256, 512], P('node'), may hold values from -6 to 6
- moment2: float32 [256, 512], P('node'), may hold values from 1 to 100
Outputs:
- quant_values: bfloat16 [8192, 512], P('local')
- quant_scales: bfloat16 [4, 8192], P(None, 'local')
- new_weights: float32 [8192, 512], P(('local', 'node'))
- new_moment1: float32 [256, 512], P('node')
- new_moment2: float32 [256, 512], P('node')
All inputs are finite; a program needn't handle non-finite values. Where the computation divides by a largest or mean magnitude, that divisor is 1e-20 or more.
Results may differ from a plain program's by a relative error of at most 0.0085.
Values may be sent and summed in bfloat16 or wider, within the bound.
A program may use at most 128 MiB of HBM per device.

v0:
```python
import jax
import jax.numpy as jnp
from jax import lax
from jax.sharding import PartitionSpec as P

bias_first = 1.0 - 0.9**10
bias_second = 1.0 - 0.999**10


def moments_update(owned, moment1, moment2):
    first = 0.9 * moment1 + 0.1 * owned
    second = 0.999 * moment2 + 0.001 * owned * owned
    tilde = first / bias_first / (jnp.sqrt(second / bias_second) + 1e-08)
    return (first, second, tilde)


def shards(grad_values, grad_exponents, proj, weights, moment1, moment2):
    exponent = grad_exponents[0]
    width, columns = (grad_values.shape[1], grad_values.shape[2])
    nblocks = exponent.shape[0]
    blocksize = columns // nblocks
    factor = jnp.transpose(jnp.exp2(exponent.astype(jnp.float32)))
    local_count = lax.axis_size("local")
    mantissa = grad_values[0].astype(jnp.float32)
    dequant = (mantissa.reshape(width, nblocks, blocksize) * factor[:, :, None]).reshape(
        width, columns
    )
    across = lax.psum_scatter(
        dequant.reshape(local_count, width // local_count, columns),
        "node",
        scatter_dimension=1,
        tiled=True,
    )
    owned_grad = lax.psum_scatter(across, "local", scatter_dimension=0, tiled=True)[0]
    partial_value = jnp.dot(
        jnp.transpose(proj),
        owned_grad,
        precision=lax.Precision.HIGHEST,
        preferred_element_type=jnp.float32,
    )
    rank_rows = moment1.shape[0]
    full_proj = lax.psum(partial_value, ("node", "local"))
    owned_proj = lax.dynamic_slice_in_dim(
        full_proj, lax.axis_index("node") * rank_rows, rank_rows, 0
    )
    raw_sq = jnp.sum(full_proj * full_proj, 0)
    first, second, tilde = moments_update(owned_proj, moment1, moment2)
    tilde_sq = lax.psum(jnp.sum(tilde * tilde, 0), "node")
    col_scale = jnp.sqrt(tilde_sq) / jnp.sqrt(raw_sq + 1e-06)
    new_weights = weights - 8.0 * owned_grad * col_scale[None, :]
    row_count = new_weights.shape[0]
    blocks = new_weights.reshape(row_count, nblocks, blocksize)
    block_max = (jnp.max(jnp.abs(blocks), 2) + 1e-06).astype(jnp.bfloat16)
    values = (
        (blocks / block_max.astype(jnp.float32)[:, :, None])
        .reshape(row_count, columns)
        .astype(jnp.bfloat16)
    )
    quant_values, quant_scales = (
        lax.all_gather(values, "node", axis=0, tiled=True),
        lax.all_gather(jnp.transpose(block_max), "node", axis=1, tiled=True),
    )
    return (quant_values, quant_scales, new_weights, first, second)


def solution(mesh):
    return jax.shard_map(
        shards,
        mesh=mesh,
        in_specs=(
            P(("node", "local"), None, None),
            P(("node", "local"), None, None),
            P(("local", "node"), None),
            P(("local", "node"), None),
            P("node", None),
            P("node", None),
        ),
        out_specs=(
            P("local", None),
            P(None, "local"),
            P(("local", "node"), None),
            P("node", None),
            P("node", None),
        ),
        check_vma=False,
    )
```

profile of v0, /device:TPU:1, one launch (start us, length us, event | category | flops | bytes accessed | tf_op | source)
XLA Modules:
  0.0 741.2 jit_solution(9300270018532788906)
XLA Ops:
  7.2 1.0 exponential_bitcast_fusion
  8.2 2.6 copy.37
  10.8 16.6 %mul.61 = f32[8192,4,128]{2,1,0:T(4,128)} broadcast(f32[8192,4]{1,0:T(8,128)} %copy.37), dimensions={0,1} | broadcast | bytes 16908288 | tf_op jit(solution)/shard_map/mul | solution.py:25
  27.4 19.9 %mul.62 = f32[8,1024,512]{2,1,0:T(8,128)} reshape(f32[8192,4,128]{2,1,0:T(4,128)} %mul.61) | data formatting | bytes 33554432 | tf_op jit(solution)/shard_map/mul | solution.py:25
  47.3 13.8 %convert_multiply_fusion = f32[8,1024,512]{2,1,0:T(8,128)} fusion(f32[8,1024,512]{2,1,0:T(8,128)} %mul.62, bf16[8,1024,512]{2,1,0:T(8,128)(2,1)} %bitcast.26), kind=kLoop, calls=%fused_computation | loop fusion | flops 8388608 | bytes 41943040 | tf_op jit(solution)/shard_map/mul | solution.py:25
  61.2 0.0 reduce-scatter.5.cloned.1.call-start
  61.2 192.1 %reduce-scatter.3.cloned.1.call-done = f32[8,32,512]{2,1,0:T(8,128)} async-done(((f32[8,1024,512]{2,1,0:T(8,128)}), f32[8,32,512]{2,1,0:T(8,128)}) %reduce-scatter.3.cloned.1.call-update) | async-done | bytes 524304 | tf_op jit(solution)/shard_map/reduce_scatter | solution.py:28
  253.4 88.5 %reduce-scatter.5.cloned.1.call-done = f32[1,32,512]{2,1,0:T(8,128)} async-done(((f32[8,32,512]{2,1,0:T(8,128)}), f32[1,32,512]{2,1,0:T(8,128)}) %reduce-scatter.5.cloned.1.call-update) | async-done | bytes 65552 | tf_op jit(solution)/shard_map/reduce_scatter | solution.py:34
  342.0 2.3 convolution_bitcast_fusion
  344.3 0.0 all-gather.3.cloned.1.call-start
  344.3 255.8 %all-reduce.2.cloned.1.call-done = f32[256,512]{1,0:T(8,128)} async-done(((f32[256,512]{1,0:T(8,128)}), f32[256,512]{1,0:T(8,128)}) %all-reduce.2.cloned.1.call-update) | async-done | bytes 524304 | tf_op jit(solution)/shard_map/psum | solution.py:42
  600.1 1.3 multiply_reduce_fusion.1
  601.5 69.2 %psum.15 = f32[512]{0:T(512)S(1)} all-reduce(f32[512]{0:T(512)S(1)} %get-tuple-element.22), channel_id=1, replica_groups=mesh['node'=32,'local'=8] {'node'}, use_global_device_ids=true, to_apply=%region_4.0 | all-reduce | flops 512 | bytes 4096 | tf_op jit(solution)/shard_map/psum | solution.py:48
  670.7 1.1 multiply_reduce_fusion
  671.8 0.9 fusion.6
  672.7 0.1 reduce_max.9
  672.8 0.1 copy.39
  672.9 0.1 copy.40
  673.0 0.1 div.35
  673.1 0.6 fusion
  673.8 43.7 %all-gather = bf16[32,32,4]{1,2,0:T(4,128)(2,1)S(1)} all-gather(bf16[1,32,4]{1,2,0:T(4,128)(2,1)S(1)} %get-tuple-element.25), channel_id=1, replica_groups=mesh['node'=32,'local'=8] {'node'}, dimensions={0}, use_global_device_ids=true | all-gather | bytes 8448 | tf_op jit(solution)/shard_map/all_gather | solution.py:61
  717.5 0.7 reshape.33
  718.2 14.2 %all-gather.3.cloned.1.call-done = bf16[1024,512]{1,0:T(8,128)(2,1)} async-done(((bf16[32,512]{1,0:T(8,128)(2,1)}), bf16[1024,512]{1,0:T(8,128)(2,1)}) %all-gather.3.cloned.1.call-update) | async-done | bytes 1048592 | tf_op jit(solution)/shard_map/all_gather | solution.py:60
  732.4 2.3 copy.47
  (20 shorter events, 0.2 us)
Async XLA Ops:
  7.2 334.8 %copy-start = (f32[32,256]{1,0:T(8,128)S(1)}, f32[32,256]{1,0:T(8,128)}, u32[]{:S(2)}) copy-start(f32[32,256]{1,0:T(8,128)} %param.8) | copy-start | bytes 98308
  7.2 246.2 %reduce-scatter.3.cloned.1.call-start = ((), (), s32[]{:S(2)}) async-start(), calls=%async_computation.2 | async-start | bytes 17301504 | tf_op jit(solution)/shard_map/reduce_scatter | solution.py:28
  61.2 539.0 %copy-start.3 = (f32[8,512]{1,0:T(8,128)S(1)}, f32[8,512]{1,0:T(8,128)}, u32[]{:S(2)}) copy-start(f32[8,512]{1,0:T(8,128)} %param.10) | copy-start | bytes 49156
  61.2 539.0 %copy-start.4 = (f32[8,512]{1,0:T(8,128)S(1)}, f32[8,512]{1,0:T(8,128)}, u32[]{:S(2)}) copy-start(f32[8,512]{1,0:T(8,128)} %param.11) | copy-start | bytes 49156
  61.2 610.6 %copy-start.2 = (f32[32,512]{1,0:T(8,128)S(1)}, f32[32,512]{1,0:T(8,128)}, u32[]{:S(2)}) copy-start(f32[32,512]{1,0:T(8,128)} %param.9) | copy-start | bytes 196612
  61.2 280.8 %reduce-scatter.5.cloned.1.call-start = ((), (), s32[]{:S(2)}) async-start(), calls=%async_computation.3 | async-start | bytes 589824 | tf_op jit(solution)/shard_map/reduce_scatter | solution.py:34
  253.4 346.7 %all-reduce.2.cloned.1.call-start = ((), (), s32[]{:S(2)}) async-start(), calls=%async_computation.4 | async-start | bytes 1048576 | tf_op jit(solution)/shard_map/psum | solution.py:42
  344.3 388.1 %all-gather.3.cloned.1.call-start = ((), (), s32[]{:S(2)}) async-start(), calls=%async_computation.5 | async-start | bytes 1081344 | tf_op jit(solution)/shard_map/all_gather | solution.py:60
  672.7 62.0 %copy-start.1 = (f32[32,512]{1,0:T(8,128)}, f32[32,512]{1,0:T(8,128)S(1)}, u32[]{:S(2)}) copy-start(f32[32,512]{1,0:T(8,128)S(1)} %get-tuple-element.34) | copy-start | bytes 196612
Sparse Core Ops, SparseCore 0:
  61.3 192.0 reduce-scatter.2
  257.2 84.6 reduce-scatter.4
  348.0 252.0 all-reduce.1
  673.9 58.4 all-gather.2
where the time goes:
time: 742 us; the launch traced here: 741 us
  waiting for transfers between devices  551 us (74%)
  blocking collectives  113 us (15%)
  local copies, waits for them, and re-layouts  42.4 us (6%)
  other arithmetic  18.8 us (3%)
  between operations  13.8 us (2%)
    psum x1, waiting for transfers between devices, shards(): full_proj = lax.psum(partial_value, ('node', 'local'))  256 us
    reduce_scatter x1, waiting for transfers between devices, shards(): lax.psum_scatter(dequant.reshape(local_count, width // local_count, colum...  192 us
    reduce_scatter x1, waiting for transfers between devices, shards(): lax.psum_scatter(across, 'local', scatter_dimension=0, tiled=True)[0]  88.5 us
    psum x1, blocking collectives, shards(): tilde_sq = lax.psum(jnp.sum(tilde * tilde, 0), 'node')  69.2 us
    all_gather x1, blocking collectives, shards(): lax.all_gather(jnp.transpose(block_max), 'node', axis=1, tiled=True)  43.7 us
    mul x2, local copies, waits for them, and re-layouts, shards(): mantissa.reshape(width, nblocks, blocksize) * factor[:, :, None]  36.5 us
  transfers between devices with their start and end apart: 4, of which 4 were waited for; matrix products, arithmetic and copies ran while one was open for 0% of the time, Pallas kernels for 0%

commit v1 on v0

v1 whole, which is shorter than its diff:
```python
import functools

import jax
import jax.numpy as jnp
from jax import lax
from jax.experimental import pallas as pl
from jax.experimental.pallas import tpu as pltpu
from jax.sharding import PartitionSpec as P

MESH = pl.DeviceIdType.MESH
BIAS1 = 1.0 - 0.9**10
BIAS2 = 1.0 - 0.999**10
F32 = jnp.float32
BF16 = jnp.bfloat16
NCOPY = 160


def kernel(
    gv, ex, proj, wts, mom1, mom2,
    o_qv, o_qs, o_nw, o_m1, o_m2,
    M0, M1, S, RA, RB, S2, RA2, RB2, G2, RG, PA, PT, PP, RP, TQ, RQ, AZ, RZ,
    MO, VS, VX, W32, WG, GG, G32, E0, E1, MI, QV, QS, NW, ONE,
    ss, rs, ls,
):
    node = lax.axis_index("node")
    local = lax.axis_index("local")
    x = lax.div(node, 8)
    zl = lax.rem(lax.div(node, 2), 4)
    c = lax.rem(node, 2)
    zh = lax.div(local, 4)
    y = lax.rem(local, 4)
    z = zh * 4 + zl
    oc = 1 - c

    def dev(dx=0, dy=0, dz=0, core=None, dzl=None):
        xx = lax.rem(x + dx, 4)
        yy = lax.rem(y + dy, 4)
        if dzl is None:
            zz = lax.rem(z + dz, 8)
        else:
            zz = zh * 4 + lax.rem(zl + dzl, 4)
        cc = c if core is None else core
        return (xx * 8 + lax.rem(zz, 4) * 2 + cc, lax.div(zz, 4) * 4 + yy)

    counter = [0]
    copies = []

    def remote(src, dst, to):
        i = counter[0]
        counter[0] += 1
        r = pltpu.make_async_remote_copy(
            src_ref=src, dst_ref=dst, send_sem=ss.at[i], recv_sem=rs.at[i],
            device_id=to, device_id_type=MESH)
        r.start()
        copies.append(r)
        return r

    lcount = [0]

    def localcopy(src, dst):
        i = lcount[0]
        lcount[0] += 1
        r = pltpu.make_async_copy(src, dst, ls.at[i])
        r.start()
        return r

    partners = [dev(core=oc)]
    partners += [dev(dx=i, dy=j) for i in range(4) for j in range(4) if (i, j) != (0, 0)]
    partners += [dev(dz=k) for k in range(1, 8)]
    partners += [dev(dzl=k, core=oc) for k in range(1, 4)]
    barrier = pltpu.get_barrier_semaphore()
    for d in partners:
        pl.semaphore_signal(barrier, inc=1, device_id=d, device_id_type=MESH)

    REL = (2, 1, 3, 0)
    ORDER = ((0, 0), (0, 1), (1, 1), (2, 0), (1, 0), (2, 1), (3, 0), (3, 1))

    def dest(k, di):
        return lax.rem((x if k == 0 else y) + REL[di], 4)

    def gslice(k, di, h, core):
        d = dest(k, di)
        rows = pl.ds(16 * k, 16)
        if k == 0:
            return gv.at[pl.ds(h * 4, 4), d, :, core, rows, :]
        return gv.at[h * 4 + d, :, :, core, rows, :]

    ld_e = localcopy(ex, E0)
    loads = {}
    for di, h in ORDER:
        for k in range(2):
            loads[k, di, h] = localcopy(gslice(k, di, h, c), M0.at[k, di, h])
    ld_w = localcopy(wts, W32)
    ld_p = localcopy(proj, PA.at[z])
    ld_m = [localcopy(mom1, MI.at[0]), localcopy(mom2, MI.at[1])]
    ONE[...] = jnp.ones((128, 128), BF16)

    pl.semaphore_wait(barrier, len(partners))

    sendE = remote(ex, E1, dev(core=oc))
    sends = {}
    for di, h in ORDER:
        for k in range(2):
            sends[k, di, h] = remote(gslice(k, di, h, oc), M1.at[k, di, h], dev(core=oc))
    pas = [remote(proj, PA.at[z], dev(dz=k)) for k in range(1, 8)]

    ld_w.wait()
    WG[x, zl, c] = W32[...].astype(BF16)

    lane = lax.broadcasted_iota(jnp.int32, (32, 128), 1)
    row = lax.broadcasted_iota(jnp.int32, (32, 128), 0)
    hit0 = row + jnp.where(row >= 16, 48, 0) + c * 32
    masks = [lane == hit0, lane == hit0 + 16]

    def dequant(k, di, h):
        d = dest(k, di)

        def body(q, carry):
            for t in range(2):
                base = (((h * 4 + q) * 4 + d) if k == 0 else ((h * 4 + d) * 4 + q)) * 256 + t * 128
                base = pl.multiple_of(base, 128)
                facs = []
                for E in (E0, E1):
                    e = E[:, pl.ds(base, 128)]
                    f = 0.5 * lax.shift_left(jnp.ones_like(e), e + 1).astype(F32)
                    lhs = jnp.concatenate(
                        [jnp.where(masks[k], f[b:b + 1, :], 0.0) for b in range(4)], 0
                    ).astype(BF16)
                    facs.append(jnp.dot(lhs, ONE[...], preferred_element_type=F32))
                for zz in range(2):
                    for b in range(4):
                        cols = pl.ds(b * 128, 128)
                        r0 = (b * 2 + zz) * 16
                        v = (
                            M0[k, di, h, q, 2 * t + zz, :, cols].astype(F32) * facs[0][r0:r0 + 16]
                            + M1[k, di, h, q, 2 * t + zz, :, cols].astype(F32) * facs[1][r0:r0 + 16]
                        )
                        S[k, di, h, q, 2 * t + zz, :, cols] = v.astype(BF16)
            return carry

        lax.fori_loop(0, 4, body, 0, unroll=2)

    def nb(k, stage, step):
        if (k + stage) % 2 == 0:
            return dev(dx=step)
        return dev(dy=step)

    ld_e.wait()
    sendE.wait_recv()
    RAc, RBc = {}, {}

    def addinto(dst, src):
        def body(i, carry):
            q, r = lax.div(i, 4), lax.rem(i, 4)
            dst[q, r] = (dst[q, r].astype(F32) + src[q, r].astype(F32)).astype(BF16)
            return carry
        lax.fori_loop(0, 16, body, 0, unroll=4)

    wx = None
    for n, (di, h) in enumerate(ORDER):
        for k in range(2):
            loads[k, di, h].wait()
            sends[k, di, h].wait_recv()
            dequant(k, di, h)
            step = 1 if h == 0 else 3
            if di == 0:
                RAc[k, h] = remote(S.at[k, 0, h], RA.at[k, h], nb(k, 0, step))
            elif (di, h) == (1, 1):
                RBc[k, 0, 1] = remote(S.at[k, 1, 1], RB.at[k, 0, 1], nb(k, 0, 1))
            elif (di, h) == (2, 0):
                RBc[k, 1, 0] = remote(S.at[k, 2, 0], RB.at[k, 1, 0], nb(k, 0, 3))
        if n == 3:
            wx = [remote(WG.at[x, zl, c], WG.at[x, zl, c], dev(dx=i)) for i in range(1, 4)]
    for h in range(2):
        for k in range(2):
            RAc[k, h].wait_recv()
            di = 1 if h == 0 else 2
            addinto(S.at[k, di, h], RA.at[k, h])
            if h == 0:
                RBc[k, 0, 0] = remote(S.at[k, 1, 0], RB.at[k, 0, 0], nb(k, 0, 1))
            else:
                RBc[k, 1, 1] = remote(S.at[k, 2, 1], RB.at[k, 1, 1], nb(k, 0, 3))

    for r in wx:
        r.wait_recv()
    wz = [remote(WG.at[:, zl, c], WG.at[:, zl, c], dev(dzl=i)) for i in range(1, 4)]

    ld_p.wait()
    for r in pas:
        r.wait_recv()
    pt = jnp.transpose(PA[...].reshape(256, 256))
    hi = pt.astype(BF16)
    rest = pt - hi.astype(F32)
    mid = rest.astype(BF16)
    PT[0] = hi
    PT[1] = mid
    PT[2] = (rest - mid.astype(F32)).astype(BF16)

    RAc2, RBc2 = {}, {}

    def finish1(k, di, h):
        a = lax.rem((y if k == 0 else x) + REL[di], 4)
        for r in range(4):
            v = (S[k, 3, h, a, r].astype(F32) + RB[k, 0, h, a, r].astype(F32)
                 + RB[k, 1, h, a, r].astype(F32))
            S2[k, di, h, r] = v.astype(BF16)

    for k in range(2):
        for s in range(2):
            for h in ((1, 0) if s == 0 else (0, 1)):
                RBc[k, s, h].wait_recv()
    for di, h in ORDER:
        for k in range(2):
            finish1(k, di, h)
            step = 1 if h == 0 else 3
            if di == 0:
                RAc2[k, h] = remote(S2.at[k, 0, h], RA2.at[k, h], nb(k, 1, step))
            elif (di, h) == (1, 1):
                RBc2[k, 0, 1] = remote(S2.at[k, 1, 1], RB2.at[k, 0, 1], nb(k, 1, 1))
            elif (di, h) == (2, 0):
                RBc2[k, 1, 0] = remote(S2.at[k, 2, 0], RB2.at[k, 1, 0], nb(k, 1, 3))
    for h in range(2):
        for k in range(2):
            RAc2[k, h].wait_recv()
            di = 1 if h == 0 else 2
            for r in range(4):
                S2[k, di, h, r] = (S2[k, di, h, r].astype(F32) + RA2[k, h, r].astype(F32)).astype(BF16)
            if h == 0:
                RBc2[k, 0, 0] = remote(S2.at[k, 1, 0], RB2.at[k, 0, 0], nb(k, 1, 1))
            else:
                RBc2[k, 1, 1] = remote(S2.at[k, 2, 1], RB2.at[k, 1, 1], nb(k, 1, 3))
    for k in range(2):
        for s in range(2):
            for h in ((1, 0) if s == 0 else (0, 1)):
                RBc2[k, s, h].wait_recv()
        for h in range(2):
            for r in range(4):
                v = (S2[k, 3, h, r].astype(F32) + RB2[k, 0, h, r].astype(F32)
                     + RB2[k, 1, h, r].astype(F32))
                G2[h * 4 + r, pl.ds(16 * k, 16), :] = v.astype(BF16)

    gz = [remote(G2.at[lax.rem(z + k, 8)], RG.at[z], dev(dz=k)) for k in (4, 3, 5, 2, 6, 1, 7)]

    g2 = G2[...].reshape(256, 512)
    part = (jnp.dot(PT[0], g2, preferred_element_type=F32)
            + jnp.dot(PT[1], g2, preferred_element_type=F32)
            + jnp.dot(PT[2], g2, preferred_element_type=F32))
    PP[...] = part.reshape(4, 4, 2, 8, 512)
    pc = remote(PP.at[:, :, oc], RP, dev(core=oc))
    pc.wait_recv()
    for i in range(4):
        for r in range(4):
            v = PP[i, r, c] + RP[i, r]
            for j in range(4):
                TQ[i, j, r] = v[:, j * 128:(j + 1) * 128]
    RQ[x, y] = TQ[x, y]
    qs = [remote(TQ.at[lax.rem(x + i, 4), lax.rem(y + j, 4)], RQ.at[x, y], dev(dx=i, dy=j))
          for i in range(4) for j in range(4) if (i, j) != (0, 0)]
    for r in qs:
        r.wait_recv()
    acc = RQ[0, 0]
    for i in range(1, 16):
        acc = acc + RQ[i // 4, i % 4]
    AZ[...] = acc
    RZ[z] = AZ[zl]
    zs = [remote(AZ.at[lax.rem(zl + k, 4)], RZ.at[z], dev(dz=k)) for k in range(1, 8)]

    for r in wz:
        r.wait_recv()
    wc = remote(WG.at[:, :, c], WG.at[:, :, c], dev(core=oc))

    for r in gz:
        r.wait_recv()
    RG[z] = G2[z]
    g = RG[0].astype(F32)
    for i in range(1, 8):
        g = g + RG[i].astype(F32)
    G32[...] = g
    GG[x, zl, c] = g.astype(BF16)
    ga = [remote(GG.at[x, zl, c], GG.at[x, zl, c], dev(dzl=i)) for i in range(1, 4)]

    for r in zs:
        r.wait_recv()
    pj = RZ[0]
    for i in range(1, 8):
        pj = pj + RZ[i]
    for r in ld_m:
        r.wait()
    ycol = pl.ds(pl.multiple_of(y * 128, 128), 128)
    first = 0.9 * MI[0, :, ycol] + 0.1 * pj
    second = 0.999 * MI[1, :, ycol] + 0.001 * pj * pj
    tilde = first / BIAS1 / (jnp.sqrt(second / BIAS2) + 1e-08)
    raw = jnp.sum(pj * pj, 0, keepdims=True)
    til = jnp.sum(tilde * tilde, 0, keepdims=True)
    r8 = lax.broadcasted_iota(jnp.int32, (8, 128), 0)
    VS[zl, c] = jnp.where(r8 == 0, raw, jnp.where(r8 == 1, til, 0.0))
    vs = [remote(VS.at[zl, c], VS.at[zl, c], dev(dzl=i, core=cc))
          for i, cc in ((2, c), (2, oc), (1, c), (3, c), (1, oc), (3, oc), (0, oc))]
    MO[y, 0] = first
    MO[y, 1] = second
    mo = [remote(MO.at[y], MO.at[y], dev(dy=i)) for i in range(1, 4)]
    for r in vs:
        r.wait_recv()
    v = VS[0, 0]
    for i in range(1, 8):
        v = v + VS[i // 2, i % 2]
    VX[x, y] = v
    vx = [remote(VX.at[x, y], VX.at[x, y], dev(dx=i, dy=j))
          for i, j in ((2, 2), (1, 2), (3, 2), (2, 1), (2, 3), (0, 2), (2, 0), (1, 1), (1, 3), (3, 1),
                       (3, 3), (0, 1), (0, 3), (1, 0), (3, 0))]
    for r in ga:
        r.wait_recv()
    gx = [remote(GG.at[x, :, c], GG.at[x, :, c], dev(dx=i)) for i in (2, 1, 3)]
    outs = []
    for r in mo:
        r.wait_recv()
    for j in range(4):
        outs.append(localcopy(MO.at[j, 0], o_m1.at[:, pl.ds(128 * j, 128)]))
        outs.append(localcopy(MO.at[j, 1], o_m2.at[:, pl.ds(128 * j, 128)]))
    for r in vx:
        r.wait_recv()
    cs = []
    for j in range(4):
        t = VX[0, j] + VX[1, j] + VX[2, j] + VX[3, j]
        cs.append(8.0 * (jnp.sqrt(t[1:2]) / jnp.sqrt(t[0:1] + 1e-06)))
    for j in range(4):
        cols = pl.ds(128 * j, 128)
        NW[:, cols] = W32[:, cols] - G32[:, cols] * cs[j]
    outs.append(localcopy(NW, o_nw))
    for r in gx:
        r.wait_recv()
    gc = remote(GG.at[:, :, c], GG.at[:, :, c], dev(core=oc))
    wc.wait_recv()
    gc.wait_recv()

    eye = (lax.broadcasted_iota(jnp.int32, (8, 128), 0)
           == lax.broadcasted_iota(jnp.int32, (8, 128), 1)).astype(BF16)
    lane32 = lax.broadcasted_iota(jnp.int32, (32, 128), 1)

    def quant(i, carry):
        stack = []
        for u in range(4):
            n = i * 4 + u
            nx, nz, nc = lax.div(n, 8), lax.rem(lax.div(n, 2), 4), u % 2
            packed = jnp.zeros((32, 128), F32)
            for j in range(4):
                cols = pl.ds(128 * j, 128)
                v = WG[nx, nz, nc, :, cols].astype(F32) - GG[nx, nz, nc, :, cols].astype(F32) * cs[j]
                scale = (jnp.max(jnp.abs(v), 1, keepdims=True) + 1e-06).astype(BF16).astype(F32)
                QV[pl.ds(pl.multiple_of(n * 32, 32), 32), cols] = (v / scale).astype(BF16)
                packed = jnp.where(lane32 == j, scale, packed)
            stack.append(packed.astype(BF16))
        st = jnp.concatenate(stack, 0)
        tr = lax.dot_general(eye, st, (((1,), (1,)), ((), ())), preferred_element_type=F32)
        QS[:, pl.ds(pl.multiple_of(i * 128, 128), 128)] = tr[:4].astype(BF16)
        return carry

    lax.fori_loop(0, 8, quant, 0)
    outs.append(localcopy(QV, o_qv))
    outs.append(localcopy(QS, o_qs))
    for r in outs:
        r.wait()
    for r in copies:
        r.wait_send()


def shards(grad_values, grad_exponents, proj, weights, moment1, moment2):
    gv = grad_values.reshape(8, 4, 4, 2, 32, 512)
    ex = grad_exponents.reshape(4, 8192)
    any_ = pl.BlockSpec(memory_space=pl.ANY)
    V = pltpu.VMEM
    scratch = [
        V((2, 4, 2, 4, 4, 16, 512), BF16),
        V((2, 4, 2, 4, 4, 16, 512), BF16),
        V((2, 4, 2, 4, 4, 16, 512), BF16),
        V((2, 2, 4, 4, 16, 512), BF16),
        V((2, 2, 2, 4, 4, 16, 512), BF16),
        V((2, 4, 2, 4, 16, 512), BF16),
        V((2, 2, 4, 16, 512), BF16),
        V((2, 2, 2, 4, 16, 512), BF16),
        V((8, 32, 512), BF16),
        V((8, 32, 512), BF16),
        V((8, 32, 256), F32),
        V((3, 256, 256), BF16),
        V((4, 4, 2, 8, 512), F32),
        V((4, 4, 8, 512), F32),
        V((4, 4, 4, 8, 128), F32),
        V((4, 4, 4, 8, 128), F32),
        V((4, 8, 128), F32),
        V((8, 8, 128), F32),
        V((4, 2, 8, 128), F32),
        V((4, 2, 8, 128), F32),
        V((4, 4, 8, 128), F32),
        V((32, 512), F32),
        V((4, 4, 2, 32, 512), BF16),
        V((4, 4, 2, 32, 512), BF16),
        V((32, 512), F32),
        V((4, 8192), jnp.int32),
        V((4, 8192), jnp.int32),
        V((2, 8, 512), F32),
        V((1024, 512), BF16),
        V((4, 1024), BF16),
        V((32, 512), F32),
        V((128, 128), BF16),
        pltpu.SemaphoreType.DMA((NCOPY,)),
        pltpu.SemaphoreType.DMA((NCOPY,)),
        pltpu.SemaphoreType.DMA((40,)),
    ]
    return pl.pallas_call(
        kernel,
        out_shape=(
            jax.ShapeDtypeStruct((1024, 512), BF16),
            jax.ShapeDtypeStruct((4, 1024), BF16),
            jax.ShapeDtypeStruct((32, 512), F32),
            jax.ShapeDtypeStruct((8, 512), F32),
            jax.ShapeDtypeStruct((8, 512), F32),
        ),
        in_specs=[any_] * 6,
        out_specs=(any_,) * 5,
        scratch_shapes=scratch,
        compiler_params=pltpu.CompilerParams(
            collective_id=0, has_side_effects=True, vmem_limit_bytes=60 * 1024 * 1024
        ),
    )(gv, ex, proj, weights, moment1, moment2)


def solution(mesh):
    return jax.shard_map(
        shards,
        mesh=mesh,
        in_specs=(
            P(("node", "local"), None, None),
            P(("node", "local"), None, None),
            P(("local", "node"), None),
            P(("local", "node"), None),
            P("node", None),
            P("node", None),
        ),
        out_specs=(
            P("local", None),
            P(None, "local"),
            P(("local", "node"), None),
            P("node", None),
            P("node", None),
        ),
        check_vma=False,
    )
```

time: 742 us -> 84 us (0.11)
  waiting for transfers between devices: 551 us -> 0 us
  blocking collectives: 113 us -> 0 us
  Pallas kernels: 0 us -> 75.3 us
  local copies, waits for them, and re-layouts: 42.4 us -> 7.68 us
  other arithmetic: 18.8 us -> 0 us
  between operations: 13.8 us -> 0.64 us
    reduce_scatter x2 -> x0, waiting for transfers between devices: 281 us -> none  [the longest x1 192 us: shards(): lax.psum_scatter(dequant.reshape(local_count, width // local_count, colum...]
    psum x1 -> x0, waiting for transfers between devices: 256 us -> none  [shards(): full_proj = lax.psum(partial_value, ('node', 'local'))]
    pallas_call x0 -> x1, Pallas kernels: none -> 75.3 us  [shards(): pl.pallas_call(kernel, out_shape=(jax.ShapeDtypeStruct((1024, 512), BF16)...]
    psum x1 -> x0, blocking collectives: 69.2 us -> none  [shards(): tilde_sq = lax.psum(jnp.sum(tilde * tilde, 0), 'node')]
    all_gather x1 -> x0, blocking collectives: 43.7 us -> none  [shards(): lax.all_gather(jnp.transpose(block_max), 'node', axis=1, tiled=True)]
    mul x2 -> x0, local copies, waits for them, and re-layouts: 36.5 us -> none  [shards(): mantissa.reshape(width, nblocks, blocksize) * factor[:, :, None]]
    all_gather x1 -> x0, waiting for transfers between devices: 14.2 us -> none  [shards(): lax.all_gather(values, 'node', axis=0, tiled=True)]
    mul x2 -> x0, other arithmetic: 13.8 us -> none  [the longest x1 13.8 us: shards(): mantissa.reshape(width, nblocks, blocksize) * factor[:, :, None]]
  transfers between devices with their start and end apart: 4 -> 0, of which waited for: 4 -> 0; matrix products, arithmetic and copies ran while one was open for 0% -> 0% of each run, Pallas kernels for 0% -> 0%
where the time goes in v1:
time: 84 us; the launch traced here: 83.6 us
  Pallas kernels  75.3 us (90%)
  local copies, waits for them, and re-layouts  7.68 us (9%)
    pallas_call x1, Pallas kernels, shards(): pl.pallas_call(kernel, out_shape=(jax.ShapeDtypeStruct((1024, 512), BF16)...  75.3 us
    unnamed x5, local copies, waits for them, and re-layouts  7.68 us

profile of v1, /device:TPU:1, one launch (start us, length us, event | category | flops | bytes accessed | tf_op | source)
XLA Modules:
  0.0 83.6 jit_solution(13951317479741046225)
XLA Ops:
  0.6 75.3 %shard_map.101 = (bf16[1024,512]{1,0:T(8,128)(2,1)}, bf16[4,1024]{1,0:T(4,128)(2,1)}, f32[32,512]{1,0:T(8,128)}, f32[8,512]{1,0:T(8,128)}, f32[8,512]{1,0:T(8,128)}) custom-call(bf16[8,4,4,2,32,512]{5,4,3,2,1,0:T(8,128)(2,1)} %bitcast.2, s32[4,8192]{1,0:T(4,128)} %bitcast.3, f32[32,256]{1,0:T(8,128)} %proj.1, f32[32,512]{1,0:T(8,128)} %wts.1, ...), custom_call_target="tpu_custom_call" | custom-call | tf_op jit(solution)/shard_map/pallas_call | solution.py:409
  75.9 2.3 %copy.16 = bf16[1024,512]{1,0:T(8,128)(2,1)} copy(bf16[1024,512]{1,0:T(8,128)(2,1)} %get-tuple-element.10) | data formatting | bytes 2097152
  78.2 1.3 %copy.17 = bf16[4,1024]{1,0:T(4,128)(2,1)} copy(bf16[4,1024]{1,0:T(4,128)(2,1)} %get-tuple-element.11) | data formatting | bytes 16384
  79.5 1.5 %copy.18 = f32[32,512]{1,0:T(8,128)} copy(f32[32,512]{1,0:T(8,128)} %get-tuple-element.12) | data formatting | bytes 131072
  81.0 1.3 %copy.19 = f32[8,512]{1,0:T(8,128)} copy(f32[8,512]{1,0:T(8,128)} %get-tuple-element.13) | data formatting | bytes 32768
  82.3 1.3 %copy.20 = f32[8,512]{1,0:T(8,128)} copy(f32[8,512]{1,0:T(8,128)} %get-tuple-element.14) | data formatting | bytes 32768

commit v2 on v1

--- a/solution.py
+++ b/solution.py
@@ -13,13 +13,14 @@
 F32 = jnp.float32
 BF16 = jnp.bfloat16
 NCOPY = 160
+PRE = 10
 
 
 def kernel(
     gv, ex, proj, wts, mom1, mom2,
-    o_qv, o_qs, o_nw, o_m1, o_m2,
+    o_wg, o_gg, o_g, o_cs, o_mo,
     M0, M1, S, RA, RB, S2, RA2, RB2, G2, RG, PA, PT, PP, RP, TQ, RQ, AZ, RZ,
-    MO, VS, VX, W32, WG, GG, G32, E0, E1, MI, QV, QS, NW, ONE,
+    MO, VS, VX, W32, WG, GG, G32, E0, E1, MI, CS, ONE,
     ss, rs, ls,
 ):
     node = lax.axis_index("node")
@@ -95,73 +96,82 @@
     ld_m = [localcopy(mom1, MI.at[0]), localcopy(mom2, MI.at[1])]
     ONE[...] = jnp.ones((128, 128), BF16)
 
-    pl.semaphore_wait(barrier, len(partners))
-
-    sendE = remote(ex, E1, dev(core=oc))
-    sends = {}
-    for di, h in ORDER:
-        for k in range(2):
-            sends[k, di, h] = remote(gslice(k, di, h, oc), M1.at[k, di, h], dev(core=oc))
-    pas = [remote(proj, PA.at[z], dev(dz=k)) for k in range(1, 8)]
-
-    ld_w.wait()
-    WG[x, zl, c] = W32[...].astype(BF16)
-
     lane = lax.broadcasted_iota(jnp.int32, (32, 128), 1)
     row = lax.broadcasted_iota(jnp.int32, (32, 128), 0)
     hit0 = row + jnp.where(row >= 16, 48, 0) + c * 32
     masks = [lane == hit0, lane == hit0 + 16]
 
-    def dequant(k, di, h):
+    def factors(E, k, di, h, q):
         d = dest(k, di)
-
-        def body(q, carry):
+        rows = []
+        for u in range(2):
             for t in range(2):
-                base = (((h * 4 + q) * 4 + d) if k == 0 else ((h * 4 + d) * 4 + q)) * 256 + t * 128
-                base = pl.multiple_of(base, 128)
-                facs = []
-                for E in (E0, E1):
-                    e = E[:, pl.ds(base, 128)]
-                    f = 0.5 * lax.shift_left(jnp.ones_like(e), e + 1).astype(F32)
-                    lhs = jnp.concatenate(
-                        [jnp.where(masks[k], f[b:b + 1, :], 0.0) for b in range(4)], 0
-                    ).astype(BF16)
-                    facs.append(jnp.dot(lhs, ONE[...], preferred_element_type=F32))
-                for zz in range(2):
+                base = (((h * 4 + q + u) * 4 + d) if k == 0 else ((h * 4 + d) * 4 + q + u)) * 256 + t * 128
+                e = E[:, pl.ds(pl.multiple_of(base, 128), 128)]
+                f = 0.5 * lax.shift_left(jnp.ones_like(e), e + 1).astype(F32)
+                rows += [jnp.where(masks[k], f[b:b + 1, :], 0.0).astype(BF16) for b in range(4)]
+        return jnp.dot(jnp.concatenate(rows, 0), ONE[...], preferred_element_type=F32).astype(BF16)
+
+    def dequant(k, di, h, E, M, add):
+        def body(p, carry):
+            q = p * 2
+            fac = factors(E, k, di, h, q)
+            for u in range(2):
+                for t in range(2):
                     for b in range(4):
-                        cols = pl.ds(b * 128, 128)
-                        r0 = (b * 2 + zz) * 16
-                        v = (
-                            M0[k, di, h, q, 2 * t + zz, :, cols].astype(F32) * facs[0][r0:r0 + 16]
-                            + M1[k, di, h, q, 2 * t + zz, :, cols].astype(F32) * facs[1][r0:r0 + 16]
-                        )
-                        S[k, di, h, q, 2 * t + zz, :, cols] = v.astype(BF16)
+                        for zz in range(2):
+                            cols = pl.ds(b * 128, 128)
+                            r0 = (((u * 2 + t) * 4 + b) * 2 + zz) * 16
+                            v = M[k, di, h, q + u, 2 * t + zz, :, cols] * fac[r0:r0 + 16]
+                            if add:
+                                v = S[k, di, h, q + u, 2 * t + zz, :, cols] + v
+                            S[k, di, h, q + u, 2 * t + zz, :, cols] = v
             return carry
 
-        lax.fori_loop(0, 4, body, 0, unroll=2)
+        lax.fori_loop(0, 2, body, 0)
+
+    ld_w.wait()
+    WG[x, zl, c] = W32[...].astype(BF16)
+    ld_e.wait()
+    UNITS = [(k, di, h) for di, h in ORDER for k in range(2)]
+    for n, (k, di, h) in enumerate(UNITS):
+        if n == PRE:
+            break
+        loads[k, di, h].wait()
+        dequant(k, di, h, E0, M0, False)
+
+    pl.semaphore_wait(barrier, len(partners))
+
+    sendE = remote(ex, E1, dev(core=oc))
+    wx = [remote(WG.at[x, zl, c], WG.at[x, zl, c], dev(dx=i)) for i in range(1, 4)]
+    sends = {}
+    for di, h in ORDER:
+        for k in range(2):
+            sends[k, di, h] = remote(gslice(k, di, h, oc), M1.at[k, di, h], dev(core=oc))
+    pas = [remote(proj, PA.at[z], dev(dz=k)) for k in range(1, 8)]
 
     def nb(k, stage, step):
         if (k + stage) % 2 == 0:
             return dev(dx=step)
         return dev(dy=step)
 
-    ld_e.wait()
+    for k, di, h in UNITS[PRE:]:
+        loads[k, di, h].wait()
+        dequant(k, di, h, E0, M0, False)
     sendE.wait_recv()
     RAc, RBc = {}, {}
 
     def addinto(dst, src):
         def body(i, carry):
             q, r = lax.div(i, 4), lax.rem(i, 4)
-            dst[q, r] = (dst[q, r].astype(F32) + src[q, r].astype(F32)).astype(BF16)
+            dst[q, r] = dst[q, r] + src[q, r]
             return carry
         lax.fori_loop(0, 16, body, 0, unroll=4)
 
-    wx = None
     for n, (di, h) in enumerate(ORDER):
         for k in range(2):
-            loads[k, di, h].wait()
             sends[k, di, h].wait_recv()
-            dequant(k, di, h)
+            dequant(k, di, h, E1, M1, True)
             step = 1 if h == 0 else 3
             if di == 0:
                 RAc[k, h] = remote(S.at[k, 0, h], RA.at[k, h], nb(k, 0, step))
@@ -170,7 +180,9 @@
             elif (di, h) == (2, 0):
                 RBc[k, 1, 0] = remote(S.at[k, 2, 0], RB.at[k, 1, 0], nb(k, 0, 3))
         if n == 3:
-            wx = [remote(WG.at[x, zl, c], WG.at[x, zl, c], dev(dx=i)) for i in range(1, 4)]
+            for r in wx:
+                r.wait_recv()
+            wz = [remote(WG.at[:, zl, c], WG.at[:, zl, c], dev(dzl=i)) for i in range(1, 4)]
     for h in range(2):
         for k in range(2):
             RAc[k, h].wait_recv()
@@ -181,9 +193,6 @@
             else:
                 RBc[k, 1, 1] = remote(S.at[k, 2, 1], RB.at[k, 1, 1], nb(k, 0, 3))
 
-    for r in wx:
-        r.wait_recv()
-    wz = [remote(WG.at[:, zl, c], WG.at[:, zl, c], dev(dzl=i)) for i in range(1, 4)]
 
     ld_p.wait()
     for r in pas:
@@ -224,7 +233,7 @@
             RAc2[k, h].wait_recv()
             di = 1 if h == 0 else 2
             for r in range(4):
-                S2[k, di, h, r] = (S2[k, di, h, r].astype(F32) + RA2[k, h, r].astype(F32)).astype(BF16)
+                S2[k, di, h, r] = S2[k, di, h, r] + RA2[k, h, r]
             if h == 0:
                 RBc2[k, 0, 0] = remote(S2.at[k, 1, 0], RB2.at[k, 0, 0], nb(k, 1, 1))
             else:
@@ -252,22 +261,23 @@
         for r in range(4):
             v = PP[i, r, c] + RP[i, r]
             for j in range(4):
-                TQ[i, j, r] = v[:, j * 128:(j + 1) * 128]
+                TQ[i, j, pl.ds(8 * r, 8), :] = v[:, j * 128:(j + 1) * 128].astype(BF16)
     RQ[x, y] = TQ[x, y]
     qs = [remote(TQ.at[lax.rem(x + i, 4), lax.rem(y + j, 4)], RQ.at[x, y], dev(dx=i, dy=j))
           for i in range(4) for j in range(4) if (i, j) != (0, 0)]
     for r in qs:
         r.wait_recv()
-    acc = RQ[0, 0]
+    acc = RQ[0, 0].astype(F32)
     for i in range(1, 16):
-        acc = acc + RQ[i // 4, i % 4]
-    AZ[...] = acc
+        acc = acc + RQ[i // 4, i % 4].astype(F32)
+    AZ[...] = acc.reshape(4, 8, 128)
     RZ[z] = AZ[zl]
     zs = [remote(AZ.at[lax.rem(zl + k, 4)], RZ.at[z], dev(dz=k)) for k in range(1, 8)]
 
     for r in wz:
         r.wait_recv()
     wc = remote(WG.at[:, :, c], WG.at[:, :, c], dev(core=oc))
+    outs = []
 
     for r in gz:
         r.wait_recv()
@@ -276,6 +286,9 @@
     for i in range(1, 8):
         g = g + RG[i].astype(F32)
     G32[...] = g
+    outs.append(localcopy(G32, o_g))
+    wc.wait_recv()
+    outs.append(localcopy(WG, o_wg))
     GG[x, zl, c] = g.astype(BF16)
     ga = [remote(GG.at[x, zl, c], GG.at[x, zl, c], dev(dzl=i)) for i in range(1, 4)]
 
@@ -284,6 +297,11 @@
     pj = RZ[0]
     for i in range(1, 8):
         pj = pj + RZ[i]
+    for r in ga:
+        r.wait_recv()
+    gr = remote(GG.at[x, :, c], GG.at[x, :, c], dev(dx=1))
+    gl = remote(GG.at[x, :, c], GG.at[x, :, c], dev(dx=3))
+    gcs = [remote(GG.at[x, :, c], GG.at[x, :, c], dev(core=oc))]
     for r in ld_m:
         r.wait()
     ycol = pl.ds(pl.multiple_of(y * 128, 128), 128)
@@ -308,60 +326,66 @@
     vx = [remote(VX.at[x, y], VX.at[x, y], dev(dx=i, dy=j))
           for i, j in ((2, 2), (1, 2), (3, 2), (2, 1), (2, 3), (0, 2), (2, 0), (1, 1), (1, 3), (3, 1),
                        (3, 3), (0, 1), (0, 3), (1, 0), (3, 0))]
-    for r in ga:
-        r.wait_recv()
-    gx = [remote(GG.at[x, :, c], GG.at[x, :, c], dev(dx=i)) for i in (2, 1, 3)]
-    outs = []
     for r in mo:
         r.wait_recv()
-    for j in range(4):
-        outs.append(localcopy(MO.at[j, 0], o_m1.at[:, pl.ds(128 * j, 128)]))
-        outs.append(localcopy(MO.at[j, 1], o_m2.at[:, pl.ds(128 * j, 128)]))
+    outs.append(localcopy(MO, o_mo))
+    xl, xr = lax.rem(x + 3, 4), lax.rem(x + 1, 4)
+    lo, hi_ = pl.ds(0, 2), pl.ds(2, 2)
+    gr.wait_recv()
+    fr = remote(GG.at[xl, lo, c], GG.at[xl, lo, c], dev(dx=1))
+    gcs.append(remote(GG.at[xl, :, c], GG.at[xl, :, c], dev(core=oc)))
+    gl.wait_recv()
+    fl = remote(GG.at[xr, hi_, c], GG.at[xr, hi_, c], dev(dx=3))
+    gcs.append(remote(GG.at[xr, :, c], GG.at[xr, :, c], dev(core=oc)))
     for r in vx:
         r.wait_recv()
-    cs = []
     for j in range(4):
         t = VX[0, j] + VX[1, j] + VX[2, j] + VX[3, j]
-        cs.append(8.0 * (jnp.sqrt(t[1:2]) / jnp.sqrt(t[0:1] + 1e-06)))
-    for j in range(4):
-        cols = pl.ds(128 * j, 128)
-        NW[:, cols] = W32[:, cols] - G32[:, cols] * cs[j]
-    outs.append(localcopy(NW, o_nw))
-    for r in gx:
-        r.wait_recv()
-    gc = remote(GG.at[:, :, c], GG.at[:, :, c], dev(core=oc))
-    wc.wait_recv()
-    gc.wait_recv()
-
-    eye = (lax.broadcasted_iota(jnp.int32, (8, 128), 0)
-           == lax.broadcasted_iota(jnp.int32, (8, 128), 1)).astype(BF16)
-    lane32 = lax.broadcasted_iota(jnp.int32, (32, 128), 1)
-
-    def quant(i, carry):
-        stack = []
-        for u in range(4):
-            n = i * 4 + u
-            nx, nz, nc = lax.div(n, 8), lax.rem(lax.div(n, 2), 4), u % 2
-            packed = jnp.zeros((32, 128), F32)
-            for j in range(4):
-                cols = pl.ds(128 * j, 128)
-                v = WG[nx, nz, nc, :, cols].astype(F32) - GG[nx, nz, nc, :, cols].astype(F32) * cs[j]
-                scale = (jnp.max(jnp.abs(v), 1, keepdims=True) + 1e-06).astype(BF16).astype(F32)
-                QV[pl.ds(pl.multiple_of(n * 32, 32), 32), cols] = (v / scale).astype(BF16)
-                packed = jnp.where(lane32 == j, scale, packed)
-            stack.append(packed.astype(BF16))
-        st = jnp.concatenate(stack, 0)
-        tr = lax.dot_general(eye, st, (((1,), (1,)), ((), ())), preferred_element_type=F32)
-        QS[:, pl.ds(pl.multiple_of(i * 128, 128), 128)] = tr[:4].astype(BF16)
-        return carry
-
-    lax.fori_loop(0, 8, quant, 0)
-    outs.append(localcopy(QV, o_qv))
-    outs.append(localcopy(QS, o_qs))
+        col = 8.0 * (jnp.sqrt(t[1:2]) / jnp.sqrt(t[0:1] + 1e-06))
+        CS[:, pl.ds(128 * j, 128)] = jnp.broadcast_to(col, (8, 128))
+    outs.append(localcopy(CS, o_cs))
+    xo = lax.rem(x + 2, 4)
+    fr.wait_recv()
+    gcs.append(remote(GG.at[xo, lo, c], GG.at[xo, lo, c], dev(core=oc)))
+    fl.wait_recv()
+    gcs.append(remote(GG.at[xo, hi_, c], GG.at[xo, hi_, c], dev(core=oc)))
+    for r in gcs:
+        r.wait_recv()
+    outs.append(localcopy(GG, o_gg))
     for r in outs:
         r.wait()
     for r in copies:
         r.wait_send()
+
+
+STEPS = 4
+ROWS = 1024 // STEPS
+
+
+def finish(wg, gg, g32, cs, mo, w32, o_qv, o_qs, o_nw, o_m1, o_m2):
+    @pl.when(pl.program_id(0) == 0)
+    def _():
+        for j in range(4):
+            cols = pl.ds(128 * j, 128)
+            o_nw[:, cols] = w32[:, cols] - g32[:, cols] * cs[0:1, cols]
+            o_m1[:, cols] = mo[j, 0]
+            o_m2[:, cols] = mo[j, 1]
+
+    eye = (lax.broadcasted_iota(jnp.int32, (8, 128), 0)
+           == lax.broadcasted_iota(jnp.int32, (8, 128), 1)).astype(BF16)
+    lane = lax.broadcasted_iota(jnp.int32, (128, 128), 1)
+    for i in range(ROWS // 128):
+        rows = pl.ds(i * 128, 128)
+        packed = jnp.zeros((128, 128), F32)
+        for j in range(4):
+            cols = pl.ds(128 * j, 128)
+            v = wg[rows, cols].astype(F32) - gg[rows, cols].astype(F32) * cs[0:1, cols]
+            scale = (jnp.max(jnp.abs(v), 1, keepdims=True) + 1e-06).astype(BF16).astype(F32)
+            o_qv[rows, cols] = (v * (1.0 / scale)).astype(BF16)
+            packed = jnp.where(lane == j, scale, packed)
+        tr = lax.dot_general(eye, packed.astype(BF16), (((1,), (1,)), ((), ())),
+                             preferred_element_type=F32)
+        o_qs[:, rows] = tr[:4].astype(BF16)
 
 
 def shards(grad_values, grad_exponents, proj, weights, moment1, moment2):
@@ -384,8 +408,8 @@
         V((3, 256, 256), BF16),
         V((4, 4, 2, 8, 512), F32),
         V((4, 4, 8, 512), F32),
-        V((4, 4, 4, 8, 128), F32),
-        V((4, 4, 4, 8, 128), F32),
+        V((4, 4, 32, 128), BF16),
+        V((4, 4, 32, 128), BF16),
         V((4, 8, 128), F32),
         V((8, 8, 128), F32),
         V((4, 2, 8, 128), F32),
@@ -398,16 +422,32 @@
         V((4, 8192), jnp.int32),
         V((4, 8192), jnp.int32),
         V((2, 8, 512), F32),
-        V((1024, 512), BF16),
-        V((4, 1024), BF16),
-        V((32, 512), F32),
+        V((8, 512), F32),
         V((128, 128), BF16),
         pltpu.SemaphoreType.DMA((NCOPY,)),
         pltpu.SemaphoreType.DMA((NCOPY,)),
         pltpu.SemaphoreType.DMA((40,)),
     ]
+    wg, gg, g32, cs, mo = pl.pallas_call(
+        kernel,
+        out_shape=(
+            jax.ShapeDtypeStruct((4, 4, 2, 32, 512), BF16),
+            jax.ShapeDtypeStruct((4, 4, 2, 32, 512), BF16),
+            jax.ShapeDtypeStruct((32, 512), F32),
+            jax.ShapeDtypeStruct((8, 512), F32),
+            jax.ShapeDtypeStruct((4, 2, 8, 128), F32),
+        ),
+        in_specs=[any_] * 6,
+        out_specs=(any_,) * 5,
+        scratch_shapes=scratch,
+        compiler_params=pltpu.CompilerParams(
+            collective_id=0, has_side_effects=True, vmem_limit_bytes=60 * 1024 * 1024
+        ),
+    )(gv, ex, proj, weights, moment1, moment2)
+    whole = lambda *shape: pl.BlockSpec(shape, lambda i: (0,) * len(shape))
     return pl.pallas_call(
-        kernel,
+        finish,
+        grid=(STEPS,),
         out_shape=(
             jax.ShapeDtypeStruct((1024, 512), BF16),
             jax.ShapeDtypeStruct((4, 1024), BF16),
@@ -415,13 +455,17 @@
             jax.ShapeDtypeStruct((8, 512), F32),
             jax.ShapeDtypeStruct((8, 512), F32),
         ),
-        in_specs=[any_] * 6,
-        out_specs=(any_,) * 5,
-        scratch_shapes=scratch,
-        compiler_params=pltpu.CompilerParams(
-            collective_id=0, has_side_effects=True, vmem_limit_bytes=60 * 1024 * 1024
-        ),
-    )(gv, ex, proj, weights, moment1, moment2)
+        in_specs=[
+            pl.BlockSpec((ROWS, 512), lambda i: (i, 0)),
+            pl.BlockSpec((ROWS, 512), lambda i: (i, 0)),
+            whole(32, 512), whole(8, 512), whole(4, 2, 8, 128), whole(32, 512),
+        ],
+        out_specs=(
+            pl.BlockSpec((ROWS, 512), lambda i: (i, 0)),
+            pl.BlockSpec((4, ROWS), lambda i: (0, i)),
+            whole(32, 512), whole(8, 512), whole(8, 512),
+        ),
+    )(wg.reshape(1024, 512), gg.reshape(1024, 512), g32, cs, mo, weights)
 
 
 def solution(mesh):

time: 84 us -> 73.9 us (0.88)
  local copies, waits for them, and re-layouts: 7.68 us -> 0 us
  Pallas kernels: 75.3 us -> 73.1 us
    unnamed x5 -> x0, local copies, waits for them, and re-layouts: 7.68 us -> none
    pallas_call x1 -> x2, Pallas kernels: 75.3 us -> 73.1 us  [the longest x1 69.1 us: shards(): pl.pallas_call(kernel, out_shape=(jax.ShapeDtypeStruct((4, 4, 2, 32, 512)...]
where the time goes in v2:
time: 73.9 us; the launch traced here: 73.8 us
  Pallas kernels  73.1 us (99%)
    pallas_call x1, Pallas kernels, shards(): pl.pallas_call(kernel, out_shape=(jax.ShapeDtypeStruct((4, 4, 2, 32, 512)...  69.1 us
    pallas_call x1, Pallas kernels, shards(): pl.pallas_call(finish, grid=(STEPS,), out_shape=(jax.ShapeDtypeStruct((10...  4.03 us

profile of v2, /device:TPU:1, one launch (start us, length us, event | category | flops | bytes accessed | tf_op | source)
XLA Modules:
  0.0 73.8 jit_solution(10524652555372566949)
XLA Ops:
  0.6 69.1 %shard_map.101 = (bf16[4,4,2,32,512]{4,3,2,1,0:T(8,128)(2,1)}, bf16[4,4,2,32,512]{4,3,2,1,0:T(8,128)(2,1)}, f32[32,512]{1,0:T(8,128)}, f32[8,512]{1,0:T(8,128)}, f32[4,2,8,128]{3,2,1,0:T(8,128)}) custom-call(bf16[8,4,4,2,32,512]{5,4,3,2,1,0:T(8,128)(2,1)} %bitcast.4, s32[4,8192]{1,0:T(4,128)} %bitcast.7, f32[32,256]{1,0:T(8,128)} %proj.1, f32[32,512]{1,0:T(8,128)} %w32.1, ...), custom_call_target="tpu_custom_call" | custom-call | tf_op jit(solution)/shard_map/pallas_call | solution.py:431
  69.7 4.0 %shard_map.102 = (bf16[1024,512]{1,0:T(8,128)(2,1)}, bf16[4,1024]{1,0:T(4,128)(2,1)}, f32[32,512]{1,0:T(8,128)}, f32[8,512]{1,0:T(8,128)}, f32[8,512]{1,0:T(8,128)}) custom-call(bf16[1024,512]{1,0:T(8,128)(2,1)} %bitcast.5, bf16[1024,512]{1,0:T(8,128)(2,1)} %bitcast.6, f32[32,512]{1,0:T(8,128)} %get-tuple-element.12.g32, f32[8,512]{1,0:T(8,128)} %get-tuple-element.13.cs, ...), custom_call_target="tpu_custom_call" | custom-call | tf_op jit(solution)/shard_map/pallas_call | solution.py:448

commit v3 on v2

--- a/solution.py
+++ b/solution.py
@@ -12,8 +12,9 @@
 BIAS2 = 1.0 - 0.999**10
 F32 = jnp.float32
 BF16 = jnp.bfloat16
-NCOPY = 160
-PRE = 10
+NCOPY = 200
+PRE = 16
+XY = 384
 
 
 def kernel(
@@ -21,6 +22,7 @@
     o_wg, o_gg, o_g, o_cs, o_mo,
     M0, M1, S, RA, RB, S2, RA2, RB2, G2, RG, PA, PT, PP, RP, TQ, RQ, AZ, RZ,
     MO, VS, VX, W32, WG, GG, G32, E0, E1, MI, CS, ONE,
+    M0Z, M1Z, SZ, RR, RL, UZ, RAZ, RBZ, VZ, RY, GZ,
     ss, rs, ls,
 ):
     node = lax.axis_index("node")
@@ -83,14 +85,25 @@
         d = dest(k, di)
         rows = pl.ds(16 * k, 16)
         if k == 0:
-            return gv.at[pl.ds(h * 4, 4), d, :, core, rows, :]
-        return gv.at[h * 4 + d, :, :, core, rows, :]
+            return gv.at[pl.ds(h * 4, 4), d, :, core, rows, pl.ds(0, XY)]
+        return gv.at[h * 4 + d, :, :, core, rows, pl.ds(0, XY)]
+
+    def zslice(dz, core):
+        t = lax.rem(z + dz, 8)
+        return gv.at[pl.ds(lax.div(t, 4) * 4, 4), :, lax.rem(t, 4), core, :, pl.ds(XY, 128)]
+
+    EVENTS = []
+    for i, (di, h) in enumerate(ORDER):
+        EVENTS += [(k, di, h) for k in range(2)]
+        EVENTS += {1: [4], 3: [3, 5], 5: [2, 6], 7: [1, 7, 0]}.get(i, [])
 
     ld_e = localcopy(ex, E0)
     loads = {}
-    for di, h in ORDER:
-        for k in range(2):
-            loads[k, di, h] = localcopy(gslice(k, di, h, c), M0.at[k, di, h])
+    for e in EVENTS:
+        if isinstance(e, int):
+            loads[e] = localcopy(zslice(e, c), M0Z.at[e])
+        else:
+            loads[e] = localcopy(gslice(*e, c), M0.at[e])
     ld_w = localcopy(wts, W32)
     ld_p = localcopy(proj, PA.at[z])
     ld_m = [localcopy(mom1, MI.at[0]), localcopy(mom2, MI.at[1])]
@@ -109,7 +122,7 @@
                 base = (((h * 4 + q + u) * 4 + d) if k == 0 else ((h * 4 + d) * 4 + q + u)) * 256 + t * 128
                 e = E[:, pl.ds(pl.multiple_of(base, 128), 128)]
                 f = 0.5 * lax.shift_left(jnp.ones_like(e), e + 1).astype(F32)
-                rows += [jnp.where(masks[k], f[b:b + 1, :], 0.0).astype(BF16) for b in range(4)]
+                rows += [jnp.where(masks[k], f[b:b + 1, :], 0.0).astype(BF16) for b in range(3)]
         return jnp.dot(jnp.concatenate(rows, 0), ONE[...], preferred_element_type=F32).astype(BF16)
 
     def dequant(k, di, h, E, M, add):
@@ -118,10 +131,10 @@
             fac = factors(E, k, di, h, q)
             for u in range(2):
                 for t in range(2):
-                    for b in range(4):
+                    for b in range(3):
                         for zz in range(2):
                             cols = pl.ds(b * 128, 128)
-                            r0 = (((u * 2 + t) * 4 + b) * 2 + zz) * 16
+                            r0 = (((u * 2 + t) * 3 + b) * 2 + zz) * 16
                             v = M[k, di, h, q + u, 2 * t + zz, :, cols] * fac[r0:r0 + 16]
                             if add:
                                 v = S[k, di, h, q + u, 2 * t + zz, :, cols] + v
@@ -130,24 +143,53 @@
 
         lax.fori_loop(0, 2, body, 0)
 
+    def dequant_z(dz, E, M, add):
+        t = lax.rem(z + dz, 8)
+        th, tl = lax.div(t, 4), lax.rem(t, 4)
+        mask = lane == row + lax.rem(tl, 2) * 64 + c * 32
+
+        def body(p, carry):
+            rows = []
+            for u in range(8):
+                base = ((th * 4 + p * 2 + u // 4) * 4 + u % 4) * 256 + lax.div(tl, 2) * 128
+                e = E[:, pl.ds(pl.multiple_of(base, 128), 128)]
+                f = 0.5 * lax.shift_left(jnp.ones_like(e), e + 1).astype(F32)
+                rows.append(jnp.where(mask, f[3:4, :], 0.0).astype(BF16))
+            fac = jnp.dot(jnp.concatenate(rows, 0), ONE[...], preferred_element_type=F32).astype(BF16)
+            for u in range(8):
+                at = (dz, p * 2 + u // 4, u % 4)
+                v = M[at] * fac[u * 32:u * 32 + 32]
+                if add:
+                    v = SZ[at] + v
+                SZ[at] = v
+            return carry
+
+        lax.fori_loop(0, 2, body, 0)
+
+    def prepass(e):
+        loads[e].wait()
+        if isinstance(e, int):
+            dequant_z(e, E0, M0Z, False)
+        else:
+            dequant(*e, E0, M0, False)
+
     ld_w.wait()
     WG[x, zl, c] = W32[...].astype(BF16)
     ld_e.wait()
-    UNITS = [(k, di, h) for di, h in ORDER for k in range(2)]
-    for n, (k, di, h) in enumerate(UNITS):
-        if n == PRE:
-            break
-        loads[k, di, h].wait()
-        dequant(k, di, h, E0, M0, False)
+    G2[:, :, pl.ds(XY, 128)] = jnp.zeros((8, 32, 128), BF16)
+    for e in EVENTS[:PRE]:
+        prepass(e)
 
     pl.semaphore_wait(barrier, len(partners))
 
     sendE = remote(ex, E1, dev(core=oc))
-    wx = [remote(WG.at[x, zl, c], WG.at[x, zl, c], dev(dx=i)) for i in range(1, 4)]
     sends = {}
-    for di, h in ORDER:
-        for k in range(2):
-            sends[k, di, h] = remote(gslice(k, di, h, oc), M1.at[k, di, h], dev(core=oc))
+    for e in EVENTS:
+        if isinstance(e, int):
+            sends[e] = remote(zslice(e, oc), M1Z.at[e], dev(core=oc))
+        else:
+            sends[e] = remote(gslice(*e, oc), M1.at[e], dev(core=oc))
+    wz = [remote(WG.at[x, zl, c], WG.at[x, zl, c], dev(dzl=i)) for i in range(1, 4)]
     pas = [remote(proj, PA.at[z], dev(dz=k)) for k in range(1, 8)]
 
     def nb(k, stage, step):
@@ -155,9 +197,8 @@
             return dev(dx=step)
         return dev(dy=step)
 
-    for k, di, h in UNITS[PRE:]:
-        loads[k, di, h].wait()
-        dequant(k, di, h, E0, M0, False)
+    for e in EVENTS[PRE:]:
+        prepass(e)
     sendE.wait_recv()
     RAc, RBc = {}, {}
 
@@ -168,21 +209,45 @@
             return carry
         lax.fori_loop(0, 16, body, 0, unroll=4)
 
-    for n, (di, h) in enumerate(ORDER):
-        for k in range(2):
-            sends[k, di, h].wait_recv()
-            dequant(k, di, h, E1, M1, True)
-            step = 1 if h == 0 else 3
-            if di == 0:
-                RAc[k, h] = remote(S.at[k, 0, h], RA.at[k, h], nb(k, 0, step))
-            elif (di, h) == (1, 1):
-                RBc[k, 0, 1] = remote(S.at[k, 1, 1], RB.at[k, 0, 1], nb(k, 0, 1))
-            elif (di, h) == (2, 0):
-                RBc[k, 1, 0] = remote(S.at[k, 2, 0], RB.at[k, 1, 0], nb(k, 0, 3))
-        if n == 3:
-            for r in wx:
-                r.wait_recv()
-            wz = [remote(WG.at[:, zl, c], WG.at[:, zl, c], dev(dzl=i)) for i in range(1, 4)]
+    def zadd(dz, src, ys):
+        def body(i, carry):
+            SZ[dz, i] = SZ[dz, i] + src[i]
+            return carry
+        lax.fori_loop(ys[0], ys[1], body, 0)
+
+    zright, zleft = dev(dz=1), dev(dz=7)
+    HALF = (pl.ds(0, 2), pl.ds(2, 2))
+
+    def wait_for(r, ref):
+        r.wait_recv()
+        return ref
+
+    for e in EVENTS:
+        sends[e].wait_recv()
+        if isinstance(e, int):
+            dequant_z(e, E1, M1Z, True)
+            if e == 4:
+                z4 = [remote(SZ.at[4, HALF[0]], RR.at[0, HALF[0]], zright),
+                      remote(SZ.at[4, HALF[1]], RL.at[0, HALF[1]], zleft)]
+            elif e == 3:
+                z3 = remote(SZ.at[3, HALF[1]], RR.at[1, HALF[1]], zright)
+            elif e == 5:
+                z5 = remote(SZ.at[5, HALF[0]], RL.at[1, HALF[0]], zleft)
+            elif e == 6:
+                zadd(3, wait_for(z4[0], RR.at[0]), (0, 2))
+                z3b = remote(SZ.at[3, HALF[0]], RR.at[1, HALF[0]], zright)
+                zadd(5, wait_for(z4[1], RL.at[0]), (2, 4))
+                z5b = remote(SZ.at[5, HALF[1]], RL.at[1, HALF[1]], zleft)
+            continue
+        k, di, h = e
+        dequant(k, di, h, E1, M1, True)
+        step = 1 if h == 0 else 3
+        if di == 0:
+            RAc[k, h] = remote(S.at[k, 0, h], RA.at[k, h], nb(k, 0, step))
+        elif (di, h) == (1, 1):
+            RBc[k, 0, 1] = remote(S.at[k, 1, 1], RB.at[k, 0, 1], nb(k, 0, 1))
+        elif (di, h) == (2, 0):
+            RBc[k, 1, 0] = remote(S.at[k, 2, 0], RB.at[k, 1, 0], nb(k, 0, 3))
     for h in range(2):
         for k in range(2):
             RAc[k, h].wait_recv()
@@ -192,7 +257,12 @@
                 RBc[k, 0, 0] = remote(S.at[k, 1, 0], RB.at[k, 0, 0], nb(k, 0, 1))
             else:
                 RBc[k, 1, 1] = remote(S.at[k, 2, 1], RB.at[k, 1, 1], nb(k, 0, 3))
-
+    z3.wait_recv()
+    zadd(2, wait_for(z3b, RR.at[1]), (0, 4))
+    z2 = remote(SZ.at[2], RR.at[2], zright)
+    z5.wait_recv()
+    zadd(6, wait_for(z5b, RL.at[1]), (0, 4))
+    z6 = remote(SZ.at[6], RL.at[2], zleft)
 
     ld_p.wait()
     for r in pas:
@@ -204,6 +274,11 @@
     PT[0] = hi
     PT[1] = mid
     PT[2] = (rest - mid.astype(F32)).astype(BF16)
+
+    zadd(1, wait_for(z2, RR.at[2]), (0, 4))
+    z1 = remote(SZ.at[1], RR.at[3], zright)
+    zadd(7, wait_for(z6, RL.at[2]), (0, 4))
+    z7 = remote(SZ.at[7], RL.at[3], zleft)
 
     RAc2, RBc2 = {}, {}
 
@@ -228,6 +303,16 @@
                 RBc2[k, 0, 1] = remote(S2.at[k, 1, 1], RB2.at[k, 0, 1], nb(k, 1, 1))
             elif (di, h) == (2, 0):
                 RBc2[k, 1, 0] = remote(S2.at[k, 2, 0], RB2.at[k, 1, 0], nb(k, 1, 3))
+    z1.wait_recv()
+    z7.wait_recv()
+    for i in range(4):
+        t = lax.rem(x + REL[i], 4)
+        for j in range(4):
+            UZ[i, j] = (SZ[0, j, t].astype(F32) + RR[3, j, t].astype(F32)
+                        + RL[3, j, t].astype(F32)).astype(BF16)
+    za = [remote(UZ.at[0, HALF[0]], RAZ.at[0], dev(dx=1)), remote(UZ.at[0, HALF[1]], RAZ.at[1], dev(dx=3))]
+    zb = [remote(UZ.at[1, HALF[1]], RBZ.at[0, HALF[1]], dev(dx=1)),
+          remote(UZ.at[2, HALF[0]], RBZ.at[1, HALF[0]], dev(dx=3))]
     for h in range(2):
         for k in range(2):
             RAc2[k, h].wait_recv()
@@ -238,6 +323,12 @@
                 RBc2[k, 0, 0] = remote(S2.at[k, 1, 0], RB2.at[k, 0, 0], nb(k, 1, 1))
             else:
                 RBc2[k, 1, 1] = remote(S2.at[k, 2, 1], RB2.at[k, 1, 1], nb(k, 1, 3))
+    za[0].wait_recv()
+    UZ[1, HALF[0]] = UZ[1, HALF[0]] + RAZ[0]
+    zb.append(remote(UZ.at[1, HALF[0]], RBZ.at[0, HALF[0]], dev(dx=1)))
+    za[1].wait_recv()
+    UZ[2, HALF[1]] = UZ[2, HALF[1]] + RAZ[1]
+    zb.append(remote(UZ.at[2, HALF[1]], RBZ.at[1, HALF[1]], dev(dx=3)))
     for k in range(2):
         for s in range(2):
             for h in ((1, 0) if s == 0 else (0, 1)):
@@ -246,9 +337,19 @@
             for r in range(4):
                 v = (S2[k, 3, h, r].astype(F32) + RB2[k, 0, h, r].astype(F32)
                      + RB2[k, 1, h, r].astype(F32))
-                G2[h * 4 + r, pl.ds(16 * k, 16), :] = v.astype(BF16)
-
-    gz = [remote(G2.at[lax.rem(z + k, 8)], RG.at[z], dev(dz=k)) for k in (4, 3, 5, 2, 6, 1, 7)]
+                G2[h * 4 + r, pl.ds(16 * k, 16), pl.ds(0, XY)] = v.astype(BF16)
+
+    for r in zb:
+        r.wait_recv()
+    VZ[...] = (UZ[3].astype(F32) + RBZ[0].astype(F32) + RBZ[1].astype(F32)).astype(BF16)
+    zy = [remote(VZ.at[lax.rem(y + i, 4)], RY.at[y], dev(dy=i)) for i in (2, 1, 3)]
+    gz = [remote(G2.at[lax.rem(z + k, 8), :, pl.ds(0, XY)], RG.at[z], dev(dz=k)) for k in (4, 3, 5, 2, 6, 1, 7)]
+    RY[y] = VZ[y]
+    for r in zy:
+        r.wait_recv()
+    gz_own = RY[0].astype(F32) + RY[1].astype(F32) + RY[2].astype(F32) + RY[3].astype(F32)
+    GZ[...] = gz_own
+    G2[z, :, pl.ds(XY, 128)] = gz_own.astype(BF16)
 
     g2 = G2[...].reshape(256, 512)
     part = (jnp.dot(PT[0], g2, preferred_element_type=F32)
@@ -274,22 +375,54 @@
     RZ[z] = AZ[zl]
     zs = [remote(AZ.at[lax.rem(zl + k, 4)], RZ.at[z], dev(dz=k)) for k in range(1, 8)]
 
+    xl, xr, xo = lax.rem(x + 3, 4), lax.rem(x + 1, 4), lax.rem(x + 2, 4)
+
+    class Gather:
+        def __init__(g, B):
+            g.B, g.cs = B, []
+            g.r, g.l = g.send(x, slice(None), 1), g.send(x, slice(None), 3)
+            g.core(x, slice(None))
+
+        def send(g, i, part, step):
+            v = g.B.at[i, :, c] if part == slice(None) else g.B.at[i, part, c]
+            return remote(v, v, dev(dx=step))
+
+        def core(g, i, part):
+            v = g.B.at[i, :, c] if part == slice(None) else g.B.at[i, part, c]
+            g.cs.append(remote(v, v, dev(core=oc)))
+
+        def forward(g):
+            g.r.wait_recv()
+            g.fr = g.send(xl, HALF[0], 1)
+            g.core(xl, slice(None))
+            g.l.wait_recv()
+            g.fl = g.send(xr, HALF[1], 3)
+            g.core(xr, slice(None))
+
+        def end(g):
+            g.fr.wait_recv()
+            g.core(xo, HALF[0])
+            g.fl.wait_recv()
+            g.core(xo, HALF[1])
+            for r in g.cs:
+                r.wait_recv()
+
     for r in wz:
         r.wait_recv()
-    wc = remote(WG.at[:, :, c], WG.at[:, :, c], dev(core=oc))
+    wgather = Gather(WG)
     outs = []
 
     for r in gz:
         r.wait_recv()
-    RG[z] = G2[z]
+    RG[z] = G2[z, :, pl.ds(0, XY)]
     g = RG[0].astype(F32)
     for i in range(1, 8):
         g = g + RG[i].astype(F32)
-    G32[...] = g
+    G32[:, pl.ds(0, XY)] = g
+    G32[:, pl.ds(XY, 128)] = GZ[...]
     outs.append(localcopy(G32, o_g))
-    wc.wait_recv()
-    outs.append(localcopy(WG, o_wg))
-    GG[x, zl, c] = g.astype(BF16)
+    GG[x, zl, c, :, pl.ds(0, XY)] = g.astype(BF16)
+    GG[x, zl, c, :, pl.ds(XY, 128)] = GZ[...].astype(BF16)
     ga = [remote(GG.at[x, zl, c], GG.at[x, zl, c], dev(dzl=i)) for i in range(1, 4)]
 
     for r in zs:
@@ -299,9 +432,8 @@
         pj = pj + RZ[i]
     for r in ga:
         r.wait_recv()
-    gr = remote(GG.at[x, :, c], GG.at[x, :, c], dev(dx=1))
-    gl = remote(GG.at[x, :, c], GG.at[x, :, c], dev(dx=3))
-    gcs = [remote(GG.at[x, :, c], GG.at[x, :, c], dev(core=oc))]
+    wgather.forward()
+    ggather = Gather(GG)
     for r in ld_m:
         r.wait()
     ycol = pl.ds(pl.multiple_of(y * 128, 128), 128)
@@ -329,14 +461,9 @@
     for r in mo:
         r.wait_recv()
     outs.append(localcopy(MO, o_mo))
-    xl, xr = lax.rem(x + 3, 4), lax.rem(x + 1, 4)
-    lo, hi_ = pl.ds(0, 2), pl.ds(2, 2)
-    gr.wait_recv()
-    fr = remote(GG.at[xl, lo, c], GG.at[xl, lo, c], dev(dx=1))
-    gcs.append(remote(GG.at[xl, :, c], GG.at[xl, :, c], dev(core=oc)))
-    gl.wait_recv()
-    fl = remote(GG.at[xr, hi_, c], GG.at[xr, hi_, c], dev(dx=3))
-    gcs.append(remote(GG.at[xr, :, c], GG.at[xr, :, c], dev(core=oc)))
+    wgather.end()
+    outs.append(localcopy(WG, o_wg))
+    ggather.forward()
     for r in vx:
         r.wait_recv()
     for j in range(4):
@@ -344,13 +471,7 @@
         col = 8.0 * (jnp.sqrt(t[1:2]) / jnp.sqrt(t[0:1] + 1e-06))
         CS[:, pl.ds(128 * j, 128)] = jnp.broadcast_to(col, (8, 128))
     outs.append(localcopy(CS, o_cs))
-    xo = lax.rem(x + 2, 4)
-    fr.wait_recv()
-    gcs.append(remote(GG.at[xo, lo, c], GG.at[xo, lo, c], dev(core=oc)))
-    fl.wait_recv()
-    gcs.append(remote(GG.at[xo, hi_, c], GG.at[xo, hi_, c], dev(core=oc)))
-    for r in gcs:
-        r.wait_recv()
+    ggather.end()
     outs.append(localcopy(GG, o_gg))
     for r in outs:
         r.wait()
@@ -394,16 +515,16 @@
     any_ = pl.BlockSpec(memory_space=pl.ANY)
     V = pltpu.VMEM
     scratch = [
-        V((2, 4, 2, 4, 4, 16, 512), BF16),
-        V((2, 4, 2, 4, 4, 16, 512), BF16),
-        V((2, 4, 2, 4, 4, 16, 512), BF16),
-        V((2, 2, 4, 4, 16, 512), BF16),
-        V((2, 2, 2, 4, 4, 16, 512), BF16),
-        V((2, 4, 2, 4, 16, 512), BF16),
-        V((2, 2, 4, 16, 512), BF16),
-        V((2, 2, 2, 4, 16, 512), BF16),
+        V((2, 4, 2, 4, 4, 16, XY), BF16),
+        V((2, 4, 2, 4, 4, 16, XY), BF16),
+        V((2, 4, 2, 4, 4, 16, XY), BF16),
+        V((2, 2, 4, 4, 16, XY), BF16),
+        V((2, 2, 2, 4, 4, 16, XY), BF16),
+        V((2, 4, 2, 4, 16, XY), BF16),
+        V((2, 2, 4, 16, XY), BF16),
+        V((2, 2, 2, 4, 16, XY), BF16),
         V((8, 32, 512), BF16),
-        V((8, 32, 512), BF16),
+        V((8, 32, XY), BF16),
         V((8, 32, 256), F32),
         V((3, 256, 256), BF16),
         V((4, 4, 2, 8, 512), F32),
@@ -424,9 +545,20 @@
         V((2, 8, 512), F32),
         V((8, 512), F32),
         V((128, 128), BF16),
+        V((8, 4, 4, 32, 128), BF16),
+        V((8, 4, 4, 32, 128), BF16),
+        V((8, 4, 4, 32, 128), BF16),
+        V((4, 4, 4, 32, 128), BF16),
+        V((4, 4, 4, 32, 128), BF16),
+        V((4, 4, 32, 128), BF16),
+        V((2, 2, 32, 128), BF16),
+        V((2, 4, 32, 128), BF16),
+        V((4, 32, 128), BF16),
+        V((4, 32, 128), BF16),
+        V((32, 128), F32),
         pltpu.SemaphoreType.DMA((NCOPY,)),
         pltpu.SemaphoreType.DMA((NCOPY,)),
-        pltpu.SemaphoreType.DMA((40,)),
+        pltpu.SemaphoreType.DMA((48,)),
     ]
     wg, gg, g32, cs, mo = pl.pallas_call(
         kernel,

time: 73.9 us -> 82.3 us (1.11)
  Pallas kernels: 73.1 us -> 81.6 us
    pallas_call x1, Pallas kernels: 69.1 us -> 77.5 us  [shards(): pl.pallas_call(kernel, out_shape=(jax.ShapeDtypeStruct((4, 4, 2, 32, 512)...]
where the time goes in v3:
time: 82.3 us; the launch traced here: 82.2 us
  Pallas kernels  81.6 us (99%)
    pallas_call x1, Pallas kernels, shards(): pl.pallas_call(kernel, out_shape=(jax.ShapeDtypeStruct((4, 4, 2, 32, 512)...  77.5 us
    pallas_call x1, Pallas kernels, shards(): pl.pallas_call(finish, grid=(STEPS,), out_shape=(jax.ShapeDtypeStruct((10...  4.03 us

profile of v3, /device:TPU:1, one launch (start us, length us, event | category | flops | bytes accessed | tf_op | source)
XLA Modules:
  0.0 82.2 jit_solution(6284210779080275258)
XLA Ops:
  0.6 77.5 %shard_map.101 = (bf16[4,4,2,32,512]{4,3,2,1,0:T(8,128)(2,1)}, bf16[4,4,2,32,512]{4,3,2,1,0:T(8,128)(2,1)}, f32[32,512]{1,0:T(8,128)}, f32[8,512]{1,0:T(8,128)}, f32[4,2,8,128]{3,2,1,0:T(8,128)}) custom-call(bf16[8,4,4,2,32,512]{5,4,3,2,1,0:T(8,128)(2,1)} %bitcast.4, s32[4,8192]{1,0:T(4,128)} %bitcast.7, f32[32,256]{1,0:T(8,128)} %proj.1, f32[32,512]{1,0:T(8,128)} %w32.1, ...), custom_call_target="tpu_custom_call" | custom-call | tf_op jit(solution)/shard_map/pallas_call | solution.py:563
  78.2 4.0 %shard_map.102 = (bf16[1024,512]{1,0:T(8,128)(2,1)}, bf16[4,1024]{1,0:T(4,128)(2,1)}, f32[32,512]{1,0:T(8,128)}, f32[8,512]{1,0:T(8,128)}, f32[8,512]{1,0:T(8,128)}) custom-call(bf16[1024,512]{1,0:T(8,128)(2,1)} %bitcast.5, bf16[1024,512]{1,0:T(8,128)(2,1)} %bitcast.6, f32[32,512]{1,0:T(8,128)} %get-tuple-element.12.g32, f32[8,512]{1,0:T(8,128)} %get-tuple-element.13.cs, ...), custom_call_target="tpu_custom_call" | custom-call | tf_op jit(solution)/shard_map/pallas_call | solution.py:580

commit v4 on v2

--- a/solution.py
+++ b/solution.py
@@ -349,16 +349,19 @@
     gcs.append(remote(GG.at[xo, lo, c], GG.at[xo, lo, c], dev(core=oc)))
     fl.wait_recv()
     gcs.append(remote(GG.at[xo, hi_, c], GG.at[xo, hi_, c], dev(core=oc)))
-    for r in gcs:
-        r.wait_recv()
-    outs.append(localcopy(GG, o_gg))
+    for i, r in ((x, gcs[0]), (xl, gcs[1]), (xr, gcs[2])):
+        r.wait_recv()
+        outs.append(localcopy(GG.at[i], o_gg.at[i]))
+    gcs[3].wait_recv()
+    gcs[4].wait_recv()
+    outs.append(localcopy(GG.at[xo], o_gg.at[xo]))
     for r in outs:
         r.wait()
     for r in copies:
         r.wait_send()
 
 
-STEPS = 4
+STEPS = 2
 ROWS = 1024 // STEPS
 
 

time: 73.9 us -> 72.6 us (0.982)
  Pallas kernels: 73.1 us -> 71.8 us
    pallas_call x1, Pallas kernels: 4.03 us -> 3.04 us  [shards(): pl.pallas_call(finish, grid=(STEPS,), out_shape=(jax.ShapeDtypeStruct((10...]
where the time goes in v4:
time: 72.6 us; the launch traced here: 72.5 us
  Pallas kernels  71.8 us (99%)
    pallas_call x1, Pallas kernels, shards(): pl.pallas_call(kernel, out_shape=(jax.ShapeDtypeStruct((4, 4, 2, 32, 512)...  68.8 us
    pallas_call x1, Pallas kernels, shards(): pl.pallas_call(finish, grid=(STEPS,), out_shape=(jax.ShapeDtypeStruct((10...  3.04 us

profile of v4, /device:TPU:1, one launch (start us, length us, event | category | flops | bytes accessed | tf_op | source)
XLA Modules:
  0.0 72.5 jit_solution(9409153354526712672)
XLA Ops:
  0.6 68.8 %shard_map.101 = (bf16[4,4,2,32,512]{4,3,2,1,0:T(8,128)(2,1)}, bf16[4,4,2,32,512]{4,3,2,1,0:T(8,128)(2,1)}, f32[32,512]{1,0:T(8,128)}, f32[8,512]{1,0:T(8,128)}, f32[4,2,8,128]{3,2,1,0:T(8,128)}) custom-call(bf16[8,4,4,2,32,512]{5,4,3,2,1,0:T(8,128)(2,1)} %bitcast.4, s32[4,8192]{1,0:T(4,128)} %bitcast.7, f32[32,256]{1,0:T(8,128)} %proj.1, f32[32,512]{1,0:T(8,128)} %w32.1, ...), custom_call_target="tpu_custom_call" | custom-call | tf_op jit(solution)/shard_map/pallas_call | solution.py:434
  69.4 3.0 %shard_map.102 = (bf16[1024,512]{1,0:T(8,128)(2,1)}, bf16[4,1024]{1,0:T(4,128)(2,1)}, f32[32,512]{1,0:T(8,128)}, f32[8,512]{1,0:T(8,128)}, f32[8,512]{1,0:T(8,128)}) custom-call(bf16[1024,512]{1,0:T(8,128)(2,1)} %bitcast.5, bf16[1024,512]{1,0:T(8,128)(2,1)} %bitcast.6, f32[32,512]{1,0:T(8,128)} %get-tuple-element.12.g32, f32[8,512]{1,0:T(8,128)} %get-tuple-element.13.cs, ...), custom_call_target="tpu_custom_call" | custom-call | tf_op jit(solution)/shard_map/pallas_call | solution.py:451

commit v5 on v4

--- a/solution.py
+++ b/solution.py
@@ -13,7 +13,7 @@
 F32 = jnp.float32
 BF16 = jnp.bfloat16
 NCOPY = 160
-PRE = 10
+PRE = 16
 
 
 def kernel(

time: 72.6 us -> 75.5 us (1.040)
  Pallas kernels: 71.8 us -> 74.7 us
    pallas_call x1, Pallas kernels: 68.8 us -> 71.7 us  [shards(): pl.pallas_call(kernel, out_shape=(jax.ShapeDtypeStruct((4, 4, 2, 32, 512)...]
where the time goes in v5:
time: 75.5 us; the launch traced here: 75.3 us
  Pallas kernels  74.7 us (99%)
    pallas_call x1, Pallas kernels, shards(): pl.pallas_call(kernel, out_shape=(jax.ShapeDtypeStruct((4, 4, 2, 32, 512)...  71.7 us
    pallas_call x1, Pallas kernels, shards(): pl.pallas_call(finish, grid=(STEPS,), out_shape=(jax.ShapeDtypeStruct((10...  3.04 us

profile of v5, /device:TPU:1, one launch (start us, length us, event | category | flops | bytes accessed | tf_op | source)
XLA Modules:
  0.0 75.3 jit_solution(4975193368262446000)
XLA Ops:
  0.6 71.7 %shard_map.101 = (bf16[4,4,2,32,512]{4,3,2,1,0:T(8,128)(2,1)}, bf16[4,4,2,32,512]{4,3,2,1,0:T(8,128)(2,1)}, f32[32,512]{1,0:T(8,128)}, f32[8,512]{1,0:T(8,128)}, f32[4,2,8,128]{3,2,1,0:T(8,128)}) custom-call(bf16[8,4,4,2,32,512]{5,4,3,2,1,0:T(8,128)(2,1)} %bitcast.4, s32[4,8192]{1,0:T(4,128)} %bitcast.7, f32[32,256]{1,0:T(8,128)} %proj.1, f32[32,512]{1,0:T(8,128)} %w32.1, ...), custom_call_target="tpu_custom_call" | custom-call | tf_op jit(solution)/shard_map/pallas_call | solution.py:434
  72.3 3.0 %shard_map.102 = (bf16[1024,512]{1,0:T(8,128)(2,1)}, bf16[4,1024]{1,0:T(4,128)(2,1)}, f32[32,512]{1,0:T(8,128)}, f32[8,512]{1,0:T(8,128)}, f32[8,512]{1,0:T(8,128)}) custom-call(bf16[1024,512]{1,0:T(8,128)(2,1)} %bitcast.5, bf16[1024,512]{1,0:T(8,128)(2,1)} %bitcast.6, f32[32,512]{1,0:T(8,128)} %get-tuple-element.12.g32, f32[8,512]{1,0:T(8,128)} %get-tuple-element.13.cs, ...), custom_call_target="tpu_custom_call" | custom-call | tf_op jit(solution)/shard_map/pallas_call | solution.py:451
